TPU v7x, 256 devices: a whole 4x4x8 slice. The times are simulated.
256 devices in a mesh: depth: 4 (over x), row: 16 (over z, y_hi), col: 4 (over y_lo, core).
Axes of the slice: x: 4, y: 4 (y_hi: 2, y_lo: 2; y = y_hi * 2 + y_lo), z: 8, core: 2. Of those that a mesh axis runs over, the one named last changes fastest.
Arguments:
- tokens: bfloat16 [768, 8192], P(('depth', 'row')), may hold values from -6 to 6
- out_grad: bfloat16 [768, 8192], P(('depth', 'row')), may hold values from -0.59765625 to 0.59765625
- gate_weight: bfloat16 [8192, 16384], P('depth', ('row', 'col')), may hold values from -0.0625 to 0.0625
- up_weight: bfloat16 [8192, 16384], P('depth', ('row', 'col')), may hold values from -0.0625 to 0.0625
- down_weight: bfloat16 [16384, 8192], P(('row', 'col'), 'depth'), may hold values from -0.046875 to 0.046875
Outputs:
- input_grad: bfloat16 [768, 8192], P(('depth', 'row', 'col'))
- gate_grad: bfloat16 [8192, 16384], P('depth', ('row', 'col'))
- up_grad: bfloat16 [8192, 16384], P('depth', ('row', 'col'))
- down_grad: bfloat16 [16384, 8192], P(('row', 'col'), 'depth')
All inputs are finite; a program needn't handle non-finite values.
Results may differ from a plain program's by a relative error of at most 0.024.
Values may be sent and summed in bfloat16 or wider, within the bound.
No kernel may reach another device: no remote copies, remote signals or barrier semaphores. Data moves between devices by JAX's collectives and lax.ppermute only.
A program may use at most 128 MiB of HBM per device.

v0:
```python
import jax
import jax.numpy as jnp
from jax import lax
from jax.sharding import PartitionSpec as P


def contract_rows(left, right):
    return lax.dot_general(
        left, right, (((0,), (0,)), ((), ())), preferred_element_type=jnp.float32
    )


def contract_cols(left, right):
    return lax.dot_general(
        left, right, (((1,), (1,)), ((), ())), preferred_element_type=jnp.float32
    )


def swiglu_terms(gate, up, hidden_grad):
    sig = jax.nn.sigmoid(gate)
    act = gate * sig
    hidden = (act * up).astype(jnp.bfloat16)
    gate_term = (hidden_grad * up * sig * (1.0 + gate * (1.0 - sig))).astype(jnp.bfloat16)
    up_term = (hidden_grad * act).astype(jnp.bfloat16)
    return (hidden, gate_term, up_term)


def block_work(tok_part, grad_part, gate_full, up_full, down_full):
    gate = jnp.dot(tok_part, gate_full, preferred_element_type=jnp.float32)
    up = jnp.dot(tok_part, up_full, preferred_element_type=jnp.float32)
    hidden_grad = contract_cols(grad_part, down_full)
    hidden, gate_term, up_term = swiglu_terms(gate, up, hidden_grad)
    partial_in = contract_cols(gate_term, gate_full) + contract_cols(up_term, up_full)
    return (hidden, gate_term, up_term, partial_in)


def on_device(tokens, out_grad, gate_weight, up_weight, down_weight):
    gate_full, up_full, down_full = (
        lax.all_gather(gate_weight, "depth", axis=0, tiled=True),
        lax.all_gather(up_weight, "depth", axis=0, tiled=True),
        lax.all_gather(down_weight, "depth", axis=1, tiled=True),
    )
    all_tok, all_grad = (
        lax.all_gather(tokens, "row", axis=0, tiled=True),
        lax.all_gather(out_grad, "row", axis=0, tiled=True),
    )
    hidden, gate_term, up_term, partial_in = block_work(
        all_tok, all_grad, gate_full, up_full, down_full
    )
    input_grad = lax.psum_scatter(
        partial_in, ("row", "col"), scatter_dimension=0, tiled=True
    ).astype(jnp.bfloat16)
    gate_grad, up_grad, down_grad = (
        lax.psum_scatter(
            contract_rows(all_tok, gate_term).astype(jnp.bfloat16),
            "depth",
            scatter_dimension=0,
            tiled=True,
        ).astype(jnp.float32),
        lax.psum_scatter(
            contract_rows(all_tok, up_term).astype(jnp.bfloat16),
            "depth",
            scatter_dimension=0,
            tiled=True,
        ).astype(jnp.float32),
        lax.psum_scatter(
            contract_rows(hidden, all_grad).astype(jnp.bfloat16),
            "depth",
            scatter_dimension=1,
            tiled=True,
        ).astype(jnp.float32),
    )
    return (
        input_grad,
        gate_grad.astype(jnp.bfloat16),
        up_grad.astype(jnp.bfloat16),
        down_grad.astype(jnp.bfloat16),
    )


def solution(mesh):
    return jax.shard_map(
        on_device,
        mesh=mesh,
        in_specs=(
            P(("depth", "row"), None),
            P(("depth", "row"), None),
            P("depth", ("row", "col")),
            P("depth", ("row", "col")),
            P(("row", "col"), "depth"),
        ),
        out_specs=(
            P(("depth", "row", "col"), None),
            P("depth", ("row", "col")),
            P("depth", ("row", "col")),
            P(("row", "col"), "depth"),
        ),
        check_vma=False,
    )
```

profile of v0, /device:TPU:2, one launch (start us, length us, event | category | flops | bytes accessed | tf_op | source)
XLA Modules:
  0.0 703.7 jit_solution(15544658315042769333)
XLA Ops:
  7.2 0.0 all-gather.16.cloned.1.call-start
  7.2 0.7 all-gather.16.cloned.1.call-update
  7.9 0.0 all-gather.14.cloned.1.call-start
  7.9 0.7 all-gather.14.cloned.1.call-update
  8.6 0.0 all-gather.10.cloned.1.call-start
  8.7 0.7 all-gather.10.cloned.1.call-update
  9.4 0.0 all-gather.12.cloned.1.call-start
  9.4 0.5 all-gather.12.cloned.1.call-update
  10.0 0.0 all-gather.8.cloned.1.call-start
  10.0 0.5 all-gather.8.cloned.1.call-update
  10.5 0.0 reduce-scatter.6.cloned.1.call-start
  10.6 103.0 %all-gather.16.cloned.1.call-done = bf16[16,12,8192]{2,1,0:T(8,128)(2,1)} async-done(((bf16[1,12,8192]{2,1,0:T(8,128)(2,1)}), bf16[16,12,8192]{2,1,0:T(8,128)(2,1)}) %all-gather.16.cloned.1.call-update) | async-done | bytes 3145744 | tf_op jit(solution)/shard_map/all_gather | solution.py:44
  113.6 3.2 reshape.11
  116.9 95.9 %all-gather.14.cloned.1.call-done = bf16[16,12,8192]{2,1,0:T(8,128)(2,1)} async-done(((bf16[1,12,8192]{2,1,0:T(8,128)(2,1)}), bf16[16,12,8192]{2,1,0:T(8,128)(2,1)}) %all-gather.14.cloned.1.call-update) | async-done | bytes 3145744 | tf_op jit(solution)/shard_map/all_gather | solution.py:45
  212.7 4.7 reshape.9
  217.4 43.8 %all-gather.10.cloned.1.call-done = bf16[8192,256]{1,0:T(8,128)(2,1)} async-done(((bf16[2048,256]{1,0:T(8,128)(2,1)}), bf16[8192,256]{1,0:T(8,128)(2,1)}) %all-gather.10.cloned.1.call-update) | async-done | bytes 4194320 | tf_op jit(solution)/shard_map/all_gather | solution.py:40
  261.3 3.2 fusion.5
  264.4 49.7 %all-gather.12.cloned.1.call-done = bf16[8192,256]{1,0:T(8,128)(2,1)} async-done(((bf16[2048,256]{1,0:T(8,128)(2,1)}), bf16[8192,256]{1,0:T(8,128)(2,1)}) %all-gather.12.cloned.1.call-update) | async-done | bytes 4194320 | tf_op jit(solution)/shard_map/all_gather | solution.py:39
  314.1 3.2 fusion.6
  317.3 49.7 %all-gather.8.cloned.1.call-done = bf16[256,8192]{1,0:T(8,128)(2,1)} async-done(((bf16[256,2048]{1,0:T(8,128)(2,1)}), bf16[256,8192]{1,0:T(8,128)(2,1)}) %all-gather.8.cloned.1.call-update) | async-done | bytes 4194320 | tf_op jit(solution)/shard_map/all_gather | solution.py:41
  367.0 5.3 multiply_convert_fusion.1
  372.3 0.0 copy-start.3
  372.3 0.6 copy-done.3
  373.0 3.2 fusion.1
  376.2 0.0 reduce-scatter.6.cloned.1.call-update
  376.2 0.0 reduce-scatter.4.cloned.1.call-start
  376.2 4.2 fusion
  380.4 0.0 copy-start.1
  380.4 0.0 reduce-scatter.4.cloned.1.call-update
  380.4 0.0 copy-start.5
  380.4 0.0 reduce-scatter.8.cloned.1.call-start
  380.5 1.8 copy-done.1
  382.3 3.3 convolution_convert_fusion
  385.5 0.0 copy-start.2
  385.5 0.0 reduce-scatter.8.cloned.1.call-update
  385.6 0.0 copy-done.5
  385.6 0.6 dynamic-slice
  386.8 0.0 copy-done.2
  386.8 0.0 copy-start
  386.8 0.0 copy-start.4
  386.8 4.4 fusion.7
  391.2 0.0 copy-done
  391.2 0.0 copy-done.4
  391.2 4.2 convolution_add_fusion
  395.4 296.2 %all-reduce.2 = bf16[192,8192]{1,0:T(8,128)(2,1)S(1)} all-reduce(f32[192,8192]{1,0:T(8,128)} %convolution_add_fusion), channel_id=2, replica_groups=mesh['depth'=4,'row'=16,'col'=4] {'row','col'}, use_global_device_ids=true, to_apply=%region_0.0.clone | all-reduce | flops 1572864 | bytes 9437184
  691.6 0.7 dynamic-slice_convert_fusion
  692.3 2.3 copy.14
  694.6 2.3 copy.13
  (3 shorter events, 0.0 us)
Async XLA Ops:
  7.2 106.4 %all-gather.16.cloned.1.call-start = ((), (), s32[]{:S(2)}) async-start(), calls=%async_computation.10 | async-start | bytes 4456448 | tf_op jit(solution)/shard_map/all_gather | solution.py:44
  7.9 204.8 %all-gather.14.cloned.1.call-start = ((), (), s32[]{:S(2)}) async-start(), calls=%async_computation.9 | async-start | bytes 4456448 | tf_op jit(solution)/shard_map/all_gather | solution.py:45
  8.6 252.6 %all-gather.10.cloned.1.call-start = ((), (), s32[]{:S(2)}) async-start(), calls=%async_computation.4 | async-start | bytes 5242880 | tf_op jit(solution)/shard_map/all_gather | solution.py:40
  9.4 304.7 %all-gather.12.cloned.1.call-start = ((), (), s32[]{:S(2)}) async-start(), calls=%async_computation.5 | async-start | bytes 5242880 | tf_op jit(solution)/shard_map/all_gather | solution.py:39
  10.0 357.0 %all-gather.8.cloned.1.call-start = ((), (), s32[]{:S(2)}) async-start(), calls=%async_computation.3 | async-start | bytes 5242880 | tf_op jit(solution)/shard_map/all_gather | solution.py:41
  10.5 681.7 %reduce-scatter.6.cloned.1.call-start = ((), (), s32[]{:S(2)}) async-start(), calls=%async_computation.7 | async-start | bytes 5242880 | tf_op jit(solution)/shard_map/reduce_scatter | solution.py:60
  372.3 0.6 copy-start.3
  376.2 318.4 %reduce-scatter.4.cloned.1.call-start = ((), (), s32[]{:S(2)}) async-start(), calls=%async_computation.6 | async-start | bytes 5242880 | tf_op jit(solution)/shard_map/reduce_scatter | solution.py:54
  380.4 1.9 copy-start.1
  380.4 5.1 copy-start.5
  380.4 316.4 %reduce-scatter.8.cloned.1.call-start = ((), (), s32[]{:S(2)}) async-start(), calls=%async_computation.8 | async-start | bytes 5242880 | tf_op jit(solution)/shard_map/reduce_scatter | solution.py:66
  385.5 1.3 copy-start.2
  386.8 4.4 copy-start
  386.8 4.4 copy-start.4
Sparse Core Ops, SparseCore 0:
  10.6 102.9 all-gather.15
  116.2 96.5 all-gather.13
  214.6 46.6 all-gather.9
  262.9 51.1 all-gather.11
  315.8 51.1 all-gather.7
  376.3 49.0 reduce-scatter.5
  428.2 49.0 reduce-scatter.3
  480.4 49.0 reduce-scatter.7
where the time goes:
time: 704 us
  waiting for transfers between devices  345 us (49%)
  blocking collectives  296 us (42%)
  matrix products  30.8 us (4%)
  local copies, waits for them, and re-layouts  16.2 us (2%)
  between operations  14.9 us (2%)
    unnamed x1, blocking collectives  296 us
    all_gather x1, waiting for transfers between devices, on_device(): lax.all_gather(tokens, 'row', axis=0, tiled=True)  103 us
    all_gather x1, waiting for transfers between devices, on_device(): lax.all_gather(out_grad, 'row', axis=0, tiled=True)  95.9 us
    all_gather x1, waiting for transfers between devices, on_device(): lax.all_gather(gate_weight, 'depth', axis=0, tiled=True)  49.7 us
    all_gather x1, waiting for transfers between devices, on_device(): lax.all_gather(down_weight, 'depth', axis=1, tiled=True)  49.7 us
    all_gather x1, waiting for transfers between devices, on_device(): lax.all_gather(up_weight, 'depth', axis=0, tiled=True)  43.8 us
    unnamed x17, local copies, waits for them, and re-layouts  15.5 us
  transfers between devices with their start and end apart: 8, of which 5 were waited for; matrix products, arithmetic and copies ran while one was open for 5% of the time, Pallas kernels for 0%

commit v1 on v0

--- a/solution.py
+++ b/solution.py
@@ -2,6 +2,19 @@
 import jax.numpy as jnp
 from jax import lax
 from jax.sharding import PartitionSpec as P
+
+
+def ring_gather(x, axis, dim):
+    ways = lax.axis_size(axis)
+    up = [(d, (d + 1) % ways) for d in range(ways)]
+    down = [(d, (d - 1) % ways) for d in range(ways)]
+    earlier, later = ([x], [x])
+    for _ in range(ways // 2):
+        earlier.append(lax.ppermute(earlier[-1], axis, up))
+    for _ in range((ways - 1) // 2):
+        later.append(lax.ppermute(later[-1], axis, down))
+    line = jnp.concatenate([*earlier[::-1], *later[1:]], axis=dim)
+    return jnp.roll(line, (lax.axis_index(axis) - ways // 2) * x.shape[dim], axis=dim)
 
 
 def contract_rows(left, right):
@@ -38,7 +51,7 @@
     gate_full, up_full, down_full = (
         lax.all_gather(gate_weight, "depth", axis=0, tiled=True),
         lax.all_gather(up_weight, "depth", axis=0, tiled=True),
-        lax.all_gather(down_weight, "depth", axis=1, tiled=True),
+        ring_gather(down_weight, "depth", 1),
     )
     all_tok, all_grad = (
         lax.all_gather(tokens, "row", axis=0, tiled=True),

time: 704 us -> 654 us (0.929)
  waiting for transfers between devices: 345 us -> 281 us
  local copies, waits for them, and re-layouts: 16.2 us -> 26.9 us
    all_gather x1, waiting for transfers between devices: 103 us -> 43.7 us  [on_device(): lax.all_gather(tokens, 'row', axis=0, tiled=True)]
    all_gather x1 -> x0, waiting for transfers between devices: 49.7 us -> none  [on_device(): lax.all_gather(down_weight, 'depth', axis=1, tiled=True)]
    ppermute x0 -> x3, waiting for transfers between devices: none -> 45.4 us  [the longest x2 45.4 us: ring_gather(): earlier.append(lax.ppermute(earlier[-1], axis, up))]
    unnamed x17 -> x28, local copies, waits for them, and re-layouts: 15.5 us -> 25.2 us
  transfers between devices with their start and end apart: 8 -> 10, of which waited for: 5 -> 6; matrix products, arithmetic and copies ran while one was open for 5% -> 7% of each run, Pallas kernels for 0% -> 0%
where the time goes in v1:
time: 654 us; the launch traced here: 653 us
  blocking collectives  296 us (45%)
  waiting for transfers between devices  281 us (43%)
  matrix products  30.3 us (5%)
  local copies, waits for them, and re-layouts  26.9 us (4%)
  between operations  14.9 us (2%)
    unnamed x1, blocking collectives  296 us
    all_gather x1, waiting for transfers between devices, on_device(): lax.all_gather(out_grad, 'row', axis=0, tiled=True)  95.9 us
    all_gather x1, waiting for transfers between devices, on_device(): lax.all_gather(gate_weight, 'depth', axis=0, tiled=True)  49.7 us
    ppermute x2, waiting for transfers between devices, ring_gather(): earlier.append(lax.ppermute(earlier[-1], axis, up))  45.4 us
    all_gather x1, waiting for transfers between devices, on_device(): lax.all_gather(up_weight, 'depth', axis=0, tiled=True)  43.8 us
    all_gather x1, waiting for transfers between devices, on_device(): lax.all_gather(tokens, 'row', axis=0, tiled=True)  43.7 us
    unnamed x28, local copies, waits for them, and re-layouts  25.2 us
    dot_general x3, matrix products, contract_cols(): lax.dot_general(left, right, (((1,), (1,)), ((), ())), preferred_element_...  13.1 us
  transfers between devices with their start and end apart: 10, of which 6 were waited for; matrix products, arithmetic and copies ran while one was open for 7% of the time, Pallas kernels for 0%

profile of v1, /device:TPU:2, one launch (start us, length us, event | category | flops | bytes accessed | tf_op | source)
XLA Modules:
  0.0 653.4 jit_solution(16608083825793458011)
XLA Ops:
  7.2 0.0 all-gather.13.cloned.1.call-start
  7.2 0.7 all-gather.13.cloned.1.call-update
  7.9 0.0 all-gather.11.cloned.1.call-start
  8.0 0.7 all-gather.11.cloned.1.call-update
  8.7 0.0 all-gather.7.cloned.1.call-start
  8.7 0.7 all-gather.7.cloned.1.call-update
  9.4 0.0 all-gather.9.cloned.1.call-start
  9.4 0.5 all-gather.9.cloned.1.call-update
  10.0 0.0 reduce-scatter.4.cloned.1.call-start
  10.0 1.6 collective-permute-start
  11.6 23.6 %collective-permute-done = bf16[256,2048]{1,0:T(8,128)(2,1)S(1)} collective-permute-done((bf16[256,2048]{1,0:T(8,128)(2,1)}, bf16[256,2048]{1,0:T(8,128)(2,1)S(1)}, u32[]{:S(2)}, u32[]{:S(2)}) %collective-permute-start) | collective-permute-done | bytes 1048608 | tf_op jit(solution)/shard_map/ppermute | solution.py:13
  35.2 1.5 collective-permute-start.1
  36.7 0.5 collective-permute-start.2
  37.2 21.8 %collective-permute-done.1 = bf16[256,2048]{1,0:T(8,128)(2,1)} collective-permute-done((bf16[256,2048]{1,0:T(8,128)(2,1)S(1)}, bf16[256,2048]{1,0:T(8,128)(2,1)}, u32[]{:S(2)}, u32[]{:S(2)}) %collective-permute-start.1) | collective-permute-done | bytes 1048608 | tf_op jit(solution)/shard_map/ppermute | solution.py:13
  59.0 2.3 constant_dynamic-update-slice_fusion.7
  61.3 1.0 constant_dynamic-update-slice_fusion.6
  62.4 1.0 constant_dynamic-update-slice_fusion.5
  63.4 1.1 constant_dynamic-update-slice_fusion.4
  64.4 2.4 constant_dynamic-update-slice_fusion.3
  66.8 1.0 constant_dynamic-update-slice_fusion.2
  67.8 1.0 constant_dynamic-update-slice_fusion.1
  68.9 1.0 constant_dynamic-update-slice_fusion
  69.9 43.7 %all-gather.13.cloned.1.call-done = bf16[16,12,8192]{2,1,0:T(8,128)(2,1)} async-done(((bf16[1,12,8192]{2,1,0:T(8,128)(2,1)}), bf16[16,12,8192]{2,1,0:T(8,128)(2,1)}) %all-gather.13.cloned.1.call-update) | async-done | bytes 3145744 | tf_op jit(solution)/shard_map/all_gather | solution.py:57
  113.6 3.2 reshape.11
  116.9 95.9 %all-gather.11.cloned.1.call-done = bf16[16,12,8192]{2,1,0:T(8,128)(2,1)} async-done(((bf16[1,12,8192]{2,1,0:T(8,128)(2,1)}), bf16[16,12,8192]{2,1,0:T(8,128)(2,1)}) %all-gather.11.cloned.1.call-update) | async-done | bytes 3145744 | tf_op jit(solution)/shard_map/all_gather | solution.py:58
  212.8 4.8 reshape.9
  217.5 43.8 %all-gather.7.cloned.1.call-done = bf16[8192,256]{1,0:T(8,128)(2,1)} async-done(((bf16[2048,256]{1,0:T(8,128)(2,1)}), bf16[8192,256]{1,0:T(8,128)(2,1)}) %all-gather.7.cloned.1.call-update) | async-done | bytes 4194320 | tf_op jit(solution)/shard_map/all_gather | solution.py:53
  261.3 3.2 fusion.11
  264.4 49.7 %all-gather.9.cloned.1.call-done = bf16[8192,256]{1,0:T(8,128)(2,1)} async-done(((bf16[2048,256]{1,0:T(8,128)(2,1)}), bf16[8192,256]{1,0:T(8,128)(2,1)}) %all-gather.9.cloned.1.call-update) | async-done | bytes 4194320 | tf_op jit(solution)/shard_map/all_gather | solution.py:52
  314.1 3.3 fusion.12
  317.5 4.5 multiply_convert_fusion.1
  322.0 0.6 copy-done.4
  322.6 3.2 fusion
  325.8 0.0 reduce-scatter.4.cloned.1.call-update
  325.9 0.0 reduce-scatter.6.cloned.1.call-start
  325.9 4.1 fusion.1
  330.0 0.0 reduce-scatter.6.cloned.1.call-update
  330.1 0.2 reduce-scatter.8.cloned.1.call-start
  330.3 1.6 copy-done.2
  331.9 3.3 convolution_convert_fusion
  335.3 0.0 reduce-scatter.8.cloned.1.call-update
  335.3 0.6 dynamic-slice
  336.6 4.4 fusion.13
  341.0 4.2 convolution_add_fusion
  345.2 296.1 %all-reduce.2 = bf16[192,8192]{1,0:T(8,128)(2,1)S(1)} all-reduce(f32[192,8192]{1,0:T(8,128)} %convolution_add_fusion), channel_id=2, replica_groups=mesh['depth'=4,'row'=16,'col'=4] {'row','col'}, use_global_device_ids=true, to_apply=%region_0.1.clone | all-reduce | flops 1572864 | bytes 9437184
  641.3 0.7 dynamic-slice_convert_fusion
  642.0 2.3 copy.13
  644.3 2.3 copy.14
  (18 shorter events, 0.0 us)
Async XLA Ops:
  7.2 55.2 %copy-start.3 = (bf16[256,2048]{1,0:T(8,128)(2,1)S(1)}, bf16[256,2048]{1,0:T(8,128)(2,1)}, u32[]{:S(2)}) copy-start(bf16[256,2048]{1,0:T(8,128)(2,1)} %param.9) | copy-start | bytes 3145732
  7.2 106.4 %all-gather.13.cloned.1.call-start = ((), (), s32[]{:S(2)}) async-start(), calls=%async_computation.9 | async-start | bytes 4456448 | tf_op jit(solution)/shard_map/all_gather | solution.py:57
  7.9 204.8 %all-gather.11.cloned.1.call-start = ((), (), s32[]{:S(2)}) async-start(), calls=%async_computation.8 | async-start | bytes 4456448 | tf_op jit(solution)/shard_map/all_gather | solution.py:58
  8.7 252.6 %all-gather.7.cloned.1.call-start = ((), (), s32[]{:S(2)}) async-start(), calls=%async_computation.3 | async-start | bytes 5242880 | tf_op jit(solution)/shard_map/all_gather | solution.py:53
  9.4 304.7 %all-gather.9.cloned.1.call-start = ((), (), s32[]{:S(2)}) async-start(), calls=%async_computation.4 | async-start | bytes 5242880 | tf_op jit(solution)/shard_map/all_gather | solution.py:52
  10.0 632.0 %reduce-scatter.4.cloned.1.call-start = ((), (), s32[]{:S(2)}) async-start(), calls=%async_computation.5 | async-start | bytes 5242880 | tf_op jit(solution)/shard_map/reduce_scatter | solution.py:67
  10.0 25.2 %collective-permute-start = (bf16[256,2048]{1,0:T(8,128)(2,1)}, bf16[256,2048]{1,0:T(8,128)(2,1)S(1)}, u32[]{:S(2)}, u32[]{:S(2)}) collective-permute-start(bf16[256,2048]{1,0:T(8,128)(2,1)} %param.9), channel_id=1, source_target_pairs={{0,64},{64,128},{128,192},{192,0},{1,65},{65,129},{129,193},{193,1... | collective-permute-start | bytes 3145736 | tf_op jit(solution)/shard_map/ppermute | solution.py:13
  35.2 23.8 %collective-permute-start.1 = (bf16[256,2048]{1,0:T(8,128)(2,1)S(1)}, bf16[256,2048]{1,0:T(8,128)(2,1)}, u32[]{:S(2)}, u32[]{:S(2)}) collective-permute-start(bf16[256,2048]{1,0:T(8,128)(2,1)S(1)} %collective-permute-done), channel_id=1, source_target_pairs={{0,64},{64,128},{128,192},{192,0},{1,65},{65,129},{129,193},{193,1... | collective-permute-start | bytes 3145736 | tf_op jit(solution)/shard_map/ppermute | solution.py:13
  36.7 26.7 %collective-permute-start.2 = (bf16[256,2048]{1,0:T(8,128)(2,1)}, bf16[256,2048]{1,0:T(8,128)(2,1)S(1)}, u32[]{:S(2)}, u32[]{:S(2)}) collective-permute-start(bf16[256,2048]{1,0:T(8,128)(2,1)} %param.9), channel_id=1, source_target_pairs={{0,192},{64,0},{128,64},{192,128},{1,193},{65,1},{129,65},{193,129... | collective-permute-start | bytes 3145736 | tf_op jit(solution)/shard_map/ppermute | solution.py:15
  314.1 3.3 copy-start.1
  322.0 0.6 copy-start.4
  325.9 318.4 %reduce-scatter.6.cloned.1.call-start = ((), (), s32[]{:S(2)}) async-start(), calls=%async_computation.6 | async-start | bytes 5242880 | tf_op jit(solution)/shard_map/reduce_scatter | solution.py:73
  330.0 1.9 copy-start.2
  330.1 5.2 copy-start.7
  330.1 316.5 %reduce-scatter.8.cloned.1.call-start = ((), (), s32[]{:S(2)}) async-start(), calls=%async_computation.7 | async-start | bytes 5242880 | tf_op jit(solution)/shard_map/reduce_scatter | solution.py:79
  335.3 1.3 copy-start.5
  336.5 4.4 copy-start
  336.6 4.4 copy-start.6
Sparse Core Ops, SparseCore 0:
  10.6 102.9 all-gather.12
  116.2 96.5 all-gather.10
  214.6 46.6 all-gather.6
  262.9 51.1 all-gather.8
  326.0 49.0 reduce-scatter.3
  377.7 49.0 reduce-scatter.5
  429.9 49.0 reduce-scatter.7
